TPU v7x, 128 devices: a whole 4x4x4 slice. The times are simulated.
128 devices in a mesh: dp: 64 (over z, y_lo, x, core), mp: 2 (over y_hi).
Axes of the slice: x: 4, y: 4 (y_hi: 2, y_lo: 2; y = y_hi * 2 + y_lo), z: 4, core: 2. Of those that a mesh axis runs over, the one named last changes fastest.
Arguments:
- images: bfloat16 [128, 197, 384], P('dp'), may hold values from -6 to 6
- routes: int32 [1, 128, 197, 2], P(None, 'dp'), may hold values from 0 to 3, all different within a row; in each aligned block of 197 rows (0 to 196, 197 to 393, ..., all dimensions but the last counted through in order) at most 104 rows name the same one
- w_qkv: bfloat16 [1, 384, 3, 384], P(None, 'dp', None, 'mp'), may hold values from -0.3125 to 0.3125
- w_proj: bfloat16 [1, 384, 384], P(None, 'mp', 'dp'), may hold values from -2 to 2
- w_in: bfloat16 [1, 4, 384, 1536], P(None, None, 'dp', 'mp'), may hold values from -0.3125 to 0.3125
- w_out: bfloat16 [1, 4, 1536, 384], P(None, None, 'mp', 'dp'), may hold values from -0.3125 to 0.3125
- w_router: bfloat16 [1, 384, 4], P(None, 'dp'), may hold values from -0.625 to 0.625
- ln_gain: bfloat16 [1, 2, 384], P(None, None, 'dp'), may hold values from 0.5 to 1.5
- ln_bias: bfloat16 [1, 2, 384], P(None, None, 'dp'), may hold values from -3 to 3
- cotangent: bfloat16 [128, 197, 384], P('dp'), may hold values from -6 to 6
Outputs:
- activations: float32 [128, 197, 384], P('dp')
- grad_images: float32 [128, 197, 384], P('dp')
- grad_qkv: float32 [1, 384, 3, 384], P(None, 'dp', None, 'mp')
- grad_proj: float32 [1, 384, 384], P(None, 'mp', 'dp')
- grad_in: float32 [1, 4, 384, 1536], P(None, None, 'dp', 'mp')
- grad_out: float32 [1, 4, 1536, 384], P(None, None, 'mp', 'dp')
- grad_router: float32 [1, 384, 4], P(None, 'dp')
- grad_gain: float32 [1, 2, 384], P(None, None, 'dp')
- grad_bias: float32 [1, 2, 384], P(None, None, 'dp')
Inputs may be any that keep to these rules, and one draw needn't show every extreme that they name: `routes`: in each block, each aligned group of 1 images names every expert in at most 104 of its tokens, and some group names some expert in exactly 104; a token's two experts differ.
All inputs are finite; a program needn't handle non-finite values.
Results may differ from a plain program's by a relative error of at most 0.024.
Values may be sent and summed in bfloat16 or wider, within the bound.
A program may use at most 128 MiB of HBM per device.

v0:
```python
import functools

import jax
import jax.numpy as jnp
from jax import lax
from jax.sharding import PartitionSpec as P
from jax.experimental import pallas as pl
from jax.experimental.pallas import tpu as pltpu

MESH = pl.DeviceIdType.MESH
LANES = 128

HD = 64
EXPERTS = 4
TOPK = 2
CAP = 104
EPSILON = 1e-06


def norm_forward(field, gain_row, shift_row):
    mean_value = jnp.mean(field, axis=-1, keepdims=True)
    centered = field - mean_value
    inverse = lax.rsqrt(jnp.mean(centered * centered, axis=-1, keepdims=True) + EPSILON)
    normed = centered * inverse
    return (normed * gain_row + shift_row, normed, inverse)


def norm_backward(grad_out, normed, inverse, gain_row):
    grad_gain = jnp.sum(grad_out * normed, axis=0)
    grad_shift = jnp.sum(grad_out, axis=0)
    scaled = grad_out * gain_row
    grad_in = inverse * (
        scaled
        - jnp.mean(scaled, axis=-1, keepdims=True)
        - normed * jnp.mean(scaled * normed, axis=-1, keepdims=True)
    )
    return (grad_in, grad_gain, grad_shift)


def slot_positions(chosen_ids):
    labels = jnp.arange(EXPERTS, dtype=jnp.int32)
    hit_counts = jnp.sum((chosen_ids[..., None] == labels).astype(jnp.int32), axis=-2)
    before = jnp.cumsum(hit_counts, axis=1) - hit_counts
    return jnp.take_along_axis(before, chosen_ids, axis=-1)


def gelu_slope(inner_pre):
    cumulative = 0.5 * (1.0 + jax.scipy.special.erf(inner_pre * 0.7071067811865476))
    density = jnp.exp(-0.5 * inner_pre * inner_pre) * 0.3989422804014327
    return cumulative + inner_pre * density


def group_of(kind):
    def chips():
        dp, mp = lax.axis_index("dp"), lax.axis_index("mp")
        return dp // 2, lambda i: (2 * i + dp % 2, mp)

    def cores():
        dp, mp = lax.axis_index("dp"), lax.axis_index("mp")
        return dp % 2, lambda i: (2 * (dp // 2) + i, mp)

    def whole():
        dp, mp = lax.axis_index("dp"), lax.axis_index("mp")
        return dp, lambda i: (i, mp)

    def pair():
        dp, mp = lax.axis_index("dp"), lax.axis_index("mp")
        return mp, lambda i: (dp, i)

    return {"chips": chips, "cores": cores, "pair": pair, "all": whole}[kind]


def exchange_kernel(m, pieces, gather, kind, x_ref, out_ref, send_sem, recv_sem, local_sem):
    me, device_of = group_of(kind)()
    step = out_ref.shape[1] // pieces
    barrier = pltpu.get_barrier_semaphore()

    def greet(k, carry):
        pl.semaphore_signal(
            barrier, inc=1, device_id=device_of(lax.rem(me + k, m)), device_id_type=MESH
        )
        return carry

    lax.fori_loop(1, m, greet, 0)
    pl.semaphore_wait(barrier, m - 1)
    own = pltpu.make_async_copy(x_ref if gather else x_ref.at[me], out_ref.at[me], local_sem)
    own.start()

    def describe(t):
        k = 1 + t // pieces
        part = pl.ds(pl.multiple_of((t % pieces) * step, step), step)
        peer = lax.rem(me + k, m)
        return pltpu.make_async_remote_copy(
            src_ref=x_ref.at[part] if gather else x_ref.at[peer, part],
            dst_ref=out_ref.at[me, part],
            send_sem=send_sem.at[t],
            recv_sem=recv_sem.at[t],
            device_id=device_of(peer),
            device_id_type=MESH,
        )

    def start(t, carry):
        describe(t).start()
        return carry

    def finish(t, carry):
        describe(t).wait()
        return carry

    count = (m - 1) * pieces
    lax.fori_loop(0, count, start, 0)
    lax.fori_loop(0, count, finish, 0)
    own.wait()


def exchange(x, m, gather, kind, collective_id, pieces=1):
    block = x.shape if gather else x.shape[1:]
    block_bytes = x.dtype.itemsize
    for d in block:
        block_bytes *= d
    count = (m - 1) * pieces
    return pl.pallas_call(
        functools.partial(exchange_kernel, m, pieces, gather, kind),
        out_shape=jax.ShapeDtypeStruct((m,) + tuple(block), x.dtype),
        in_specs=[pl.BlockSpec(memory_space=pl.ANY)],
        out_specs=pl.BlockSpec(memory_space=pl.ANY),
        scratch_shapes=[
            pltpu.SemaphoreType.DMA((count,)),
            pltpu.SemaphoreType.DMA((count,)),
            pltpu.SemaphoreType.DMA(()),
        ],
        compiler_params=pltpu.CompilerParams(collective_id=collective_id, has_side_effects=True),
        cost_estimate=pl.CostEstimate(flops=0, bytes_accessed=2 * m * block_bytes, transcendentals=0),
    )(x)


def relay_gather_kernel(chips, direct, x_ref, out_ref, sa, ra, sb, rb, sf, rf, sp, rp, sl):
    dp, mp = lax.axis_index("dp"), lax.axis_index("mp")
    n = 2 * chips
    core = dp % 2
    other = 1 - core
    chip = dp // 2
    barrier = pltpu.get_barrier_semaphore()

    def greet(k, carry):
        pl.semaphore_signal(
            barrier, inc=1, device_id=(lax.rem(dp + k, n), mp), device_id_type=MESH
        )
        return carry

    lax.fori_loop(1, n, greet, 0)
    pl.semaphore_wait(barrier, n - 1)
    own = pltpu.make_async_copy(x_ref, out_ref.at[dp], sl)
    own.start()

    def remote(src, dst, send, recv, target):
        return pltpu.make_async_remote_copy(
            src_ref=src, dst_ref=dst, send_sem=send, recv_sem=recv,
            device_id=(target, mp), device_id_type=MESH,
        )

    def same(j):
        return remote(x_ref, out_ref.at[dp], sa.at[j], ra.at[j], 2 * lax.rem(chip + j, chips) + core)

    def cross(j):
        return remote(x_ref, out_ref.at[dp], sb.at[j], rb.at[j], 2 * lax.rem(chip + j, chips) + other)

    def relay(j):
        slot = 2 * lax.rem(chip + chips - j, chips) + core
        return remote(out_ref.at[slot], out_ref.at[slot], sf.at[j], rf.at[j], 2 * chip + other)

    mate = remote(x_ref, out_ref.at[dp], sp, rp, 2 * chip + other)
    forwarded = [j for j in range(1, chips) if j not in direct]
    mate.start()
    for j in forwarded:
        same(j).start()
    for j in direct:
        cross(j).start()
    for j in direct:
        same(j).start()
    for j in forwarded:
        same(j).wait_recv()
        relay(j).start()
    for j in direct:
        same(j).wait_recv()
    for j in range(1, chips):
        same(j).wait_send()
    for j in direct:
        cross(j).wait()
    mate.wait()
    for j in forwarded:
        relay(j).wait()
    own.wait()


def relay_gather(x, n, collective_id):
    chips = n // 2
    direct = tuple(j for j in range(1, chips) if j % 4 == 0)
    block_bytes = x.dtype.itemsize
    for d in x.shape:
        block_bytes *= d
    return pl.pallas_call(
        functools.partial(relay_gather_kernel, chips, direct),
        out_shape=jax.ShapeDtypeStruct((n,) + tuple(x.shape), x.dtype),
        in_specs=[pl.BlockSpec(memory_space=pl.ANY)],
        out_specs=pl.BlockSpec(memory_space=pl.ANY),
        scratch_shapes=[pltpu.SemaphoreType.DMA((chips,))] * 6
        + [pltpu.SemaphoreType.DMA(())] * 3,
        compiler_params=pltpu.CompilerParams(collective_id=collective_id, has_side_effects=True),
        cost_estimate=pl.CostEstimate(flops=0, bytes_accessed=2 * n * block_bytes, transcendentals=0),
    )(x)


def relay_reduce_kernel(chips, direct, y_ref, out_same, out_cross, pin, sbuf, ss, rs, sc, rc, sr, rr, sl):
    dp, mp = lax.axis_index("dp"), lax.axis_index("mp")
    n = 2 * chips
    core = dp % 2
    other = 1 - core
    chip = dp // 2
    mate_id = 2 * chip + other
    barrier = pltpu.get_barrier_semaphore()

    def greet(k, carry):
        pl.semaphore_signal(
            barrier, inc=1, device_id=(lax.rem(dp + k, n), mp), device_id_type=MESH
        )
        return carry

    lax.fori_loop(1, n, greet, 0)
    pl.semaphore_wait(barrier, n - 1)
    own = pltpu.make_async_copy(y_ref.at[dp], out_same.at[0], sl)
    own.start()

    def remote(src, dst, send, recv, target):
        return pltpu.make_async_remote_copy(
            src_ref=src, dst_ref=dst, send_sem=send, recv_sem=recv,
            device_id=(target, mp), device_id_type=MESH,
        )

    def target(j, c):
        return 2 * lax.rem(chip + j, chips) + c

    slot_of = {j: i + 1 for i, j in enumerate(direct)}
    forwarded = [j for j in range(1, chips) if j not in direct]

    def same(j):
        src = y_ref.at[target(j, core)] if j in direct else sbuf.at[j]
        return remote(src, out_same.at[j], ss.at[j], rs.at[j], target(j, core))

    def cross(j):
        i = slot_of[j]
        return remote(y_ref.at[target(j, other)], out_cross.at[i], sc.at[i], rc.at[i], target(j, other))

    def relay(j):
        return remote(y_ref.at[target(j, other)], pin.at[j], sr.at[j], rr.at[j], mate_id)

    mate = remote(y_ref.at[mate_id], out_cross.at[0], sc.at[0], rc.at[0], mate_id)
    for j in forwarded:
        relay(j).start()
    mate.start()
    for j in direct:
        cross(j).start()
        same(j).start()
    for j in forwarded:
        relay(j).wait_recv()
        total = y_ref[target(j, core)].astype(jnp.float32) + pin[j].astype(jnp.float32)
        sbuf[j] = total.astype(sbuf.dtype)
        same(j).start()
    for j in forwarded:
        relay(j).wait_send()
    for j in range(1, chips):
        same(j).wait()
    for j in direct:
        cross(j).wait()
    mate.wait()
    own.wait()


def relay_reduce(y, n, collective_id):
    chips = n // 2
    direct = tuple(j for j in range(1, chips) if j % 4 == 0)
    block = tuple(y.shape[1:])
    block_bytes = y.dtype.itemsize
    for d in block:
        block_bytes *= d
    same, cross = pl.pallas_call(
        functools.partial(relay_reduce_kernel, chips, direct),
        out_shape=(
            jax.ShapeDtypeStruct((chips,) + block, y.dtype),
            jax.ShapeDtypeStruct((len(direct) + 1,) + block, y.dtype),
        ),
        in_specs=[pl.BlockSpec(memory_space=pltpu.VMEM)],
        out_specs=(pl.BlockSpec(memory_space=pl.ANY), pl.BlockSpec(memory_space=pl.ANY)),
        scratch_shapes=[pltpu.VMEM((chips,) + block, y.dtype)] * 2
        + [pltpu.SemaphoreType.DMA((chips,))] * 6
        + [pltpu.SemaphoreType.DMA(())],
        compiler_params=pltpu.CompilerParams(collective_id=collective_id, has_side_effects=True),
        cost_estimate=pl.CostEstimate(flops=0, bytes_accessed=3 * n * block_bytes, transcendentals=0),
    )(y)
    return jnp.sum(same.astype(jnp.float32), axis=0) + jnp.sum(cross.astype(jnp.float32), axis=0)


def padded_rows(size, dtype_rows=16):
    rows = -(-size // LANES)
    return -(-rows // dtype_rows) * dtype_rows


def shard_sizes(w_qkv, w_proj, w_in, w_out, w_router, ln_gain, ln_bias):
    return [a.size for a in (w_qkv, w_proj, w_in, w_out, w_router, ln_gain, ln_bias)]


def gather_weights(w_qkv, w_proj, w_in, w_out, w_router, ln_gain, ln_bias, n):
    parts = (w_qkv, w_proj, w_in, w_out, w_router, ln_gain, ln_bias)
    flat = jnp.concatenate([a.reshape(-1) for a in parts])
    total = flat.shape[0]
    rows = padded_rows(total)
    flat = jnp.pad(flat, (0, rows * LANES - total)).reshape(rows, LANES)
    full = relay_gather(flat, n, 0).reshape(n, rows * LANES)
    pieces = []
    start = 0
    for a in parts:
        pieces.append(full[:, start:start + a.size].reshape((n,) + a.shape[1:]))
        start += a.size
    q, p, i, o, r, g, b = pieces
    gq = q.reshape((-1,) + w_qkv.shape[2:])
    gr = r.reshape((-1,) + w_router.shape[2:])
    gg = g.transpose(1, 0, 2).reshape(ln_gain.shape[1], -1)
    gb = b.transpose(1, 0, 2).reshape(ln_bias.shape[1], -1)
    return (gq, p, i, o, gr, gg, gb)


def scatter_grads(grads, n, shapes):
    gq, gp, gi, go, gr, gg, gb = grads
    rows = [
        gq.reshape(n, -1),
        gp.reshape(n, -1),
        gi.reshape(n, -1),
        go.reshape(n, -1),
        gr.reshape(n, -1),
        gg.reshape(gg.shape[0], n, -1).transpose(1, 0, 2).reshape(n, -1),
        gb.reshape(gb.shape[0], n, -1).transpose(1, 0, 2).reshape(n, -1),
    ]
    packed = jnp.concatenate(rows, axis=1)
    total = packed.shape[1]
    count = padded_rows(total)
    packed = jnp.pad(packed, ((0, 0), (0, count * LANES - total))).reshape(n, count, LANES)
    mine = relay_reduce(packed.astype(jnp.bfloat16), n, 1).reshape(-1)
    outs = []
    start = 0
    for shape in shapes:
        size = 1
        for d in shape:
            size *= d
        outs.append(mine[start:start + size].reshape(shape))
        start += size
    return outs


def layer_forward(field, chosen_ids, weights):
    w_qkv, w_proj, w_in, w_out, w_router, ln_gain, ln_bias = weights
    image_count, length, model_width = field.shape
    row_count = image_count * length
    head_count = w_qkv.shape[2] // HD
    score_scale = HD ** (-0.5)
    gain_rows = ln_gain.astype(jnp.float32)
    shift_rows = ln_bias.astype(jnp.float32)
    flat = field.reshape(row_count, model_width)
    first, normed_one, inverse_one = norm_forward(flat, gain_rows[0], shift_rows[0])
    first = first.astype(jnp.bfloat16)
    projected = jnp.einsum("rd,dcf->rcf", first, w_qkv, preferred_element_type=jnp.float32).astype(
        jnp.bfloat16
    )
    projected = projected.reshape(image_count, length, 3, head_count, HD)
    queries = projected[:, :, 0]
    key_rows = projected[:, :, 1]
    value_rows = projected[:, :, 2]
    scores = (
        jnp.einsum("bqhe,bkhe->bhqk", queries, key_rows, preferred_element_type=jnp.float32)
        * score_scale
    )
    log_total = jax.nn.logsumexp(scores, axis=-1)
    attn_weights = jnp.exp(scores - log_total[..., None]).astype(jnp.bfloat16)
    attended = jnp.einsum(
        "bhqk,bkhe->bqhe", attn_weights, value_rows, preferred_element_type=jnp.float32
    )
    attended = attended.astype(jnp.bfloat16).reshape(row_count, head_count * HD)
    partial_attn = jnp.einsum(
        "rf,jfk->rjk", attended, w_proj, preferred_element_type=jnp.float32
    ).reshape(row_count, model_width)
    hidden = flat + lax.psum(partial_attn, "mp")
    second, normed_two, inverse_two = norm_forward(hidden, gain_rows[1], shift_rows[1])
    second = second.astype(jnp.bfloat16)
    logits = jnp.dot(second, w_router, preferred_element_type=jnp.float32)
    router = jax.nn.softmax(logits, axis=-1)
    labels = jnp.arange(EXPERTS, dtype=jnp.int32)
    ids_flat = chosen_ids.reshape(row_count, TOPK)
    chosen = (ids_flat[:, :, None] == labels).astype(jnp.float32)
    gate_values = jnp.sum(router[:, None, :] * chosen, axis=-1)
    per_image = EXPERTS * CAP
    image_base = (jnp.arange(image_count, dtype=jnp.int32) * per_image)[:, None, None]
    slot_index = (chosen_ids * CAP + slot_positions(chosen_ids) + image_base).reshape(-1)
    owners = (
        jnp.full((image_count * per_image,), row_count, jnp.int32)
        .at[slot_index]
        .set(jnp.repeat(jnp.arange(row_count, dtype=jnp.int32), TOPK))
    )
    slot_gate = (
        jnp.zeros((image_count * per_image,), jnp.float32).at[slot_index].set(gate_values.reshape(-1))
    )
    padded = jnp.concatenate([second, jnp.zeros((1, model_width), jnp.bfloat16)], axis=0)
    slot_rows = jnp.take(padded, owners, axis=0).reshape(image_count, EXPERTS, CAP, model_width)
    slot_split = slot_rows.reshape(slot_rows.shape[:3] + w_in.shape[:1] + w_in.shape[2:3])
    inner_pre = jnp.einsum("becjk,jekf->becf", slot_split, w_in, preferred_element_type=jnp.float32)
    activated = jax.nn.gelu(inner_pre, approximate=False).astype(jnp.bfloat16)
    produced = jnp.einsum("becf,jefk->becjk", activated, w_out, preferred_element_type=jnp.float32)
    produced = produced.reshape(image_count * per_image, model_width)
    picked = jnp.take(produced, slot_index, axis=0).reshape(row_count, TOPK, model_width)
    partial_moe = jnp.sum(gate_values[:, :, None] * picked, axis=1)
    output = hidden + lax.psum(partial_moe.astype(jnp.bfloat16), "mp").astype(jnp.float32)
    record = (
        normed_one, inverse_one, first, projected, log_total, attended, normed_two, inverse_two,
        second, router, chosen, slot_index, owners, slot_gate, slot_rows, inner_pre, activated, picked,
    )
    return (output.reshape(image_count, length, model_width), record)


def layer_backward(grad_field, record, weights):
    w_qkv, w_proj, w_in, w_out, w_router, ln_gain, ln_bias = weights
    (
        normed_one, inverse_one, first, projected, log_total, attended, normed_two, inverse_two,
        second, router, chosen, slot_index, owners, slot_gate, slot_rows, inner_pre, activated, picked,
    ) = record
    image_count, length, model_width = grad_field.shape
    row_count = image_count * length
    head_count = projected.shape[3]
    score_scale = HD ** (-0.5)
    gain_rows = ln_gain.astype(jnp.float32)
    grad_flat = grad_field.reshape(row_count, model_width)
    padded_grad = jnp.concatenate([grad_flat, jnp.zeros((1, model_width), jnp.float32)], axis=0)
    grad_slots = (jnp.take(padded_grad, owners, axis=0) * slot_gate[:, None]).astype(jnp.bfloat16)
    split = (w_out.shape[0], w_out.shape[3])
    grad_slots = grad_slots.reshape((image_count, EXPERTS, CAP) + split)
    slot_split = slot_rows.reshape((image_count, EXPERTS, CAP) + split)
    grad_w_out = jnp.einsum(
        "becf,becjk->jefk", activated, grad_slots, preferred_element_type=jnp.float32
    )
    grad_act = jnp.einsum("becjk,jefk->becf", grad_slots, w_out, preferred_element_type=jnp.float32)
    grad_inner = (grad_act * gelu_slope(inner_pre)).astype(jnp.bfloat16)
    grad_w_in = jnp.einsum(
        "becjk,becf->jekf", slot_split, grad_inner, preferred_element_type=jnp.float32
    )
    grad_slot_rows = jnp.einsum(
        "becf,jekf->becjk", grad_inner, w_in, preferred_element_type=jnp.float32
    )
    grad_slot_rows = grad_slot_rows.reshape(image_count * EXPERTS * CAP, model_width)
    partial_second = jnp.sum(
        jnp.take(grad_slot_rows, slot_index, axis=0).reshape(row_count, TOPK, model_width), axis=1
    )
    partial_gate = jnp.sum(picked * grad_flat[:, None, :], axis=-1)
    grad_second, grad_gate = lax.psum((partial_second, partial_gate), "mp")
    grad_router = jnp.sum(grad_gate[:, :, None] * chosen, axis=1)
    grad_logits = router * (grad_router - jnp.sum(router * grad_router, axis=-1, keepdims=True))
    grad_logits = grad_logits.astype(jnp.bfloat16)
    grad_w_router = jnp.dot(second.T, grad_logits, preferred_element_type=jnp.float32)
    grad_second = grad_second + jnp.dot(grad_logits, w_router.T, preferred_element_type=jnp.float32)
    grad_from_norm, grad_gain_two, grad_shift_two = norm_backward(
        grad_second, normed_two, inverse_two, gain_rows[1]
    )
    grad_hidden = grad_flat + grad_from_norm
    grad_hidden_low = grad_hidden.astype(jnp.bfloat16)
    grad_hidden_split = grad_hidden_low.reshape((row_count,) + split)
    grad_w_proj = jnp.einsum(
        "rf,rjk->jfk", attended, grad_hidden_split, preferred_element_type=jnp.float32
    )
    grad_attended = jnp.einsum(
        "rjk,jfk->rf", grad_hidden_split, w_proj, preferred_element_type=jnp.float32
    ).astype(jnp.bfloat16)
    grad_attended = grad_attended.reshape(image_count, length, head_count, HD)
    queries = projected[:, :, 0]
    key_rows = projected[:, :, 1]
    value_rows = projected[:, :, 2]
    scores = (
        jnp.einsum("bqhe,bkhe->bhqk", queries, key_rows, preferred_element_type=jnp.float32)
        * score_scale
    )
    probs = jnp.exp(scores - log_total[..., None])
    grad_values = jnp.einsum(
        "bhqk,bqhe->bkhe", probs.astype(jnp.bfloat16), grad_attended,
        preferred_element_type=jnp.float32,
    )
    grad_probs = jnp.einsum(
        "bqhe,bkhe->bhqk", grad_attended, value_rows, preferred_element_type=jnp.float32
    )
    grad_scores = (
        probs * (grad_probs - jnp.sum(probs * grad_probs, axis=-1, keepdims=True))
    ).astype(jnp.bfloat16)
    grad_queries = (
        jnp.einsum("bhqk,bkhe->bqhe", grad_scores, key_rows, preferred_element_type=jnp.float32)
        * score_scale
    )
    grad_keys = (
        jnp.einsum("bhqk,bqhe->bkhe", grad_scores, queries, preferred_element_type=jnp.float32)
        * score_scale
    )
    grad_projected = jnp.stack([grad_queries, grad_keys, grad_values], axis=2).astype(jnp.bfloat16)
    grad_projected = grad_projected.reshape(row_count, 3, head_count * HD)
    grad_w_qkv = jnp.einsum(
        "rd,rcf->dcf", first, grad_projected, preferred_element_type=jnp.float32
    )
    partial_first = jnp.einsum(
        "rcf,dcf->rd", grad_projected, w_qkv, preferred_element_type=jnp.float32
    )
    grad_first = lax.psum(partial_first.astype(jnp.bfloat16), "mp").astype(jnp.float32)
    grad_input_norm, grad_gain_one, grad_shift_one = norm_backward(
        grad_first, normed_one, inverse_one, gain_rows[0]
    )
    grad_input = grad_hidden + grad_input_norm
    grads = (
        grad_w_qkv,
        grad_w_proj,
        grad_w_in,
        grad_w_out,
        grad_w_router,
        jnp.stack([grad_gain_one, grad_gain_two]),
        jnp.stack([grad_shift_one, grad_shift_two]),
    )
    return (grad_input.reshape(image_count, length, model_width), grads)


def make_local(n):
    def local(images, routes, w_qkv, w_proj, w_in, w_out, w_router, ln_gain, ln_bias, cotangent):
        shapes = [a.shape for a in (w_qkv, w_proj, w_in, w_out, w_router, ln_gain, ln_bias)]
        weights = gather_weights(w_qkv, w_proj, w_in, w_out, w_router, ln_gain, ln_bias, n)
        field = images.astype(jnp.float32)
        output, record = layer_forward(field, routes[0], weights)
        grad_input, grads = layer_backward(cotangent.astype(jnp.float32), record, weights)
        shards = scatter_grads(grads, n, [(1,) + tuple(s[1:]) for s in shapes])
        return (output, grad_input, *shards)

    return local


def solution(mesh):
    n = mesh.shape["dp"]
    in_specs = (
        P("dp", None, None),
        P(None, "dp", None, None),
        P(None, "dp", None, "mp"),
        P(None, "mp", "dp"),
        P(None, None, "dp", "mp"),
        P(None, None, "mp", "dp"),
        P(None, "dp", None),
        P(None, None, "dp"),
        P(None, None, "dp"),
        P("dp", None, None),
    )
    out_specs = (
        P("dp", None, None),
        P("dp", None, None),
        P(None, "dp", None, "mp"),
        P(None, "mp", "dp"),
        P(None, None, "dp", "mp"),
        P(None, None, "mp", "dp"),
        P(None, "dp", None),
        P(None, None, "dp"),
        P(None, None, "dp"),
    )
    return jax.shard_map(make_local(n), mesh=mesh, in_specs=in_specs, out_specs=out_specs, check_vma=False)
```

profile of v0, /device:TPU:1, one launch (start us, length us, event | category | flops | bytes accessed | tf_op | source)
XLA Modules:
  0.0 459.0 jit_solution(9240861814264180684)
XLA Ops:
  15.5 58.9 %shard_map.169 = bf16[64,336,128]{2,1,0:T(8,128)(2,1)} custom-call(bf16[336,128]{1,0:T(8,128)(2,1)} %pad_bitcast_fusion.1.x_ref), custom_call_target="tpu_custom_call" | custom-call | bytes 11010048 | tf_op jit(solution)/shard_map/pallas_call | solution.py:202
  74.5 4.0 copy.476
  78.7 2.3 copy-done.2
  91.1 11.3 %all-reduce.12.cloned.1.call-start = ((), (), s32[]{:S(2)}) async-start(), calls=%async_computation.1 | async-start | bytes 1228800 | tf_op jit(solution)/shard_map/psum | solution.py:460
  102.5 5.0 %fusion.97 = (bf16[64,18432]{1,0:T(8,128)(2,1)}, bf16[64,18432]{1,0:T(8,128)(2,1)}) fusion(bf16[64,43008]{1,0:T(8,128)(2,1)} %bitcast.225), kind=kLoop, calls=%fused_computation.191 | loop fusion | bytes 9437184 | tf_op jit(solution)/shard_map/slice | solution.py:322
  107.5 2.4 reduce-window.6
  111.3 12.6 %gather_fusion.2 = s32[788]{0:T(1024)S(1)} fusion(s32[2,197,4]{1,2,0:T(4,128)S(1)} %slice_subtract_fusion, s32[788]{0:T(1024)S(1)} %reshape.552), kind=kCustom, calls=%fused_computation.4 | custom fusion | bytes 15760 | tf_op jit(solution)/shard_map/jit(take_along_axis)/gather | solution.py:44
  123.9 5.3 %scatter_custom_fusion = s32[832]{0:T(1024)S(1)} fusion(s32[788]{0:T(1024)S(1)} %fusion.89, s32[788]{0:T(1024)S(1)} %reshape.562, s32[]{:T(128)} %constant.38.clone.1), kind=kCustom, calls=%fused_computation.180 | custom fusion | bytes 3332 | tf_op jit(solution)/shard_map/scatter | solution.py:405
  132.7 6.0 %reshape.490 = bf16[64,4,6,768]{3,2,1,0:T(8,128)(2,1)} reshape(bf16[64,18432]{1,0:T(8,128)(2,1)} %get-tuple-element.78) | data formatting | bytes 4718592 | tf_op jit(solution)/shard_map/reshape | solution.py:322
  138.7 5.7 %copy.312 = bf16[64,18432]{0,1:T(8,128)(2,1)} copy(bf16[64,18432]{1,0:T(8,128)(2,1)} %get-tuple-element.79) | data formatting | bytes 4718592 | tf_op jit(solution)/shard_map/slice | solution.py:322
  144.4 9.5 %reshape.489 = bf16[64,4,768,6]{0,3,2,1:T(8,128)(2,1)} reshape(bf16[64,18432]{0,1:T(8,128)(2,1)} %copy.312) | data formatting | bytes 4718592 | tf_op jit(solution)/shard_map/reshape | solution.py:322
  157.6 3.4 gather_fusion.1
  162.8 2.8 gather.29
  170.2 3.9 gather_fusion
  177.3 9.9 %fusion.6 = (bf16[2,4,104,768]{3,2,0,1:T(8,128)(2,1)S(1)}, f32[4,768,2,104,1]{1,3,4,2,0:T(8,128)}) fusion(bf16[64,4,6,768,1]{3,2,1,0,4:T(8,128)(2,1)} %bitcast.232, bf16[2,4,104,64,6]{2,1,0,4,3:T(4,128)(2,1)} %gather.26, pred[2,4,104]{2,1,0:T(4,128)(4,1)S(1)} %copy-done.50), kind=kOutput, calls=%fused_computation.20 | convolution fusion | flops 532586496 | bytes 6832960 | tf_op jit(solution)/shard_map/becjk,jekf->becf/dot_general | solution.py:413
  187.2 4.7 %fusion.37 = f32[2,4,104,64,6]{2,3,0,4,1:T(8,128)S(1)} fusion(bf16[64,4,768,6,1]{0,3,2,1,4:T(8,128)(2,1)} %bitcast.228, bf16[2,4,104,768]{3,2,0,1:T(8,128)(2,1)S(1)} %get-tuple-element.95), kind=kOutput, calls=%fused_computation.59 | convolution fusion | flops 490733568 | bytes 4915200 | tf_op jit(solution)/shard_map/becf,jefk->becjk/dot_general | solution.py:415
  191.9 2.2 copy.319
  194.0 3.2 reshape.494
  199.0 3.4 gather_fusion.3
  202.5 2.9 multiply_reduce_fusion.1
  205.6 12.7 %psum.38 = f32[394,2]{1,0:T(8,128)S(1)} all-reduce(f32[394,2]{1,0:T(8,128)S(1)} %reduce_sum.229), channel_id=1, replica_groups=mesh['dp'=64,'mp'=2] {'mp'}, use_global_device_ids=true, to_apply=%region_20.22 | all-reduce | flops 788 | bytes 6304 | tf_op jit(solution)/shard_map/psum | solution.py:460
  219.3 5.8 %scatter_custom_fusion.1 = f32[832]{0:T(1024)S(1)} fusion(s32[788]{0:T(1024)} %copy-done.53, f32[788]{0:T(1024)S(1)} %reshape.570, f32[]{:T(128)} %constant.56.clone.1), kind=kCustom, calls=%fused_computation.178 | custom fusion | bytes 3840 | tf_op jit(solution)/shard_map/scatter | solution.py:408
  225.2 4.3 fusion.47
  229.6 5.4 %fusion.43 = bf16[2,4,104,768,1]{3,2,0,4,1:T(8,128)(2,1)S(1)} fusion(f32[4,768,2,104,1]{1,3,4,2,0:T(8,128)S(1)} %copy-done.55, bf16[64,4,768,6,1]{0,3,2,1,4:T(8,128)(2,1)} %bitcast.229, f32[2,4,104,64,6]{2,1,0,4,3:T(4,128)S(1)} %copy-done.4, f32[2,4,104]{2,1,0:T(4,128)S(1)} %mul.267, pred[2,4,104]{2,1,0:T(4,128)(4,1)S(1)} %copy-done.51), kind=kOutput, calls=%fused_computation.61 | convolution fusion | flops 498081792 | bytes 7475264 | tf_op jit(solution)/shard_map/becjk,jefk->becf/dot_general | solution.py:447
  234.9 2.7 fusion.40
  237.6 2.2 copy.328
  239.8 3.2 reshape.500
  244.8 3.7 gather_fusion.4
  251.8 3.6 reduce_sum.227
  257.9 3.3 copy.477
  261.2 7.1 %copy.349 = bf16[64,4,768,6]{0,3,2,1:T(8,128)(2,1)} copy(bf16[64,4,768,6]{2,0,3,1:T(8,128)(2,1)} %bitcast.227) | data formatting | bytes 4718592 | tf_op jit(solution)/shard_map/becf,becjk->jefk/transpose | solution.py:444
  268.3 9.5 %reshape.508 = bf16[64,18432]{0,1:T(8,128)(2,1)} reshape(bf16[64,4,768,6]{0,3,2,1:T(8,128)(2,1)} %copy.349) | data formatting | bytes 4718592 | tf_op jit(solution)/shard_map/reshape | solution.py:338
  277.8 6.0 %copy.358 = bf16[64,18432]{1,0:T(8,128)(2,1)} copy(bf16[64,18432]{0,1:T(8,128)(2,1)} %reshape.508) | data formatting | bytes 4718592 | tf_op jit(solution)/shard_map/reshape | solution.py:338
  283.8 2.2 fusion.27
  286.0 3.1 copy.347
  289.1 5.6 %reshape.507 = bf16[64,18432]{1,0:T(8,128)(2,1)} reshape(bf16[64,4,6,768]{3,2,1,0:T(8,128)(2,1)} %copy.347) | data formatting | bytes 4718592 | tf_op jit(solution)/shard_map/reshape | solution.py:337
  294.8 2.2 multiply_reduce_fusion.2
  297.0 2.2 multiply_reduce_fusion.3
  314.4 3.3 constant_dynamic-update-slice_fusion.4
  321.1 32.7 %all-reduce.14.cloned.1.call-done = (bf16[394,384]{1,0:T(8,128)(2,1)}, bf16[394,384]{1,0:T(8,128)(2,1)}) async-done(((bf16[394,384]{1,0:T(8,128)(2,1)}, bf16[394,384]{1,0:T(8,128)(2,1)}), (bf16[394,384]{1,0:T(8,128)(2,1)}, bf16[394,384]{1,0:T(8,128)(2,1)})) %all-reduce.14.cloned.1.call-update) | async-done | bytes 605200 | tf_op jit(solution)/shard_map/psum | solution.py:419
  360.0 2.9 pad_bitcast_fusion
  362.9 3.3 copy.398
  366.2 58.5 %shard_map.170 = (bf16[32,336,128]{2,1,0:T(8,128)(2,1)}, bf16[8,336,128]{2,1,0:T(8,128)(2,1)}) custom-call(bf16[64,336,128]{2,1,0:T(8,128)(2,1)} %bitcast.220), custom_call_target="tpu_custom_call" | custom-call | bytes 16515072 | tf_op jit(solution)/shard_map/pallas_call | solution.py:286
  424.7 2.2 convert_reduce_fusion
  427.1 5.1 %add.238 = f32[1792,6,4]{2,1,0:T(8,128)} reshape(f32[336,128]{1,0:T(8,128)S(1)} %add.237) | data formatting | bytes 344064 | tf_op jit(solution)/shard_map/add | solution.py:300
  432.2 7.6 %add.239 = f32[3584,2,6]{2,1,0:T(2,128)} reshape(f32[336,128]{1,0:T(8,128)S(1)} %add.237) | data formatting | bytes 344064 | tf_op jit(solution)/shard_map/add | solution.py:300
  441.8 2.7 reshape.515
  444.6 2.5 copy.365
  (322 shorter events, 78.2 us)
Async XLA Ops:
  7.2 159.8 %all-reduce.10.cloned.1.call-start = ((), (), s32[]{:S(2)}) async-start(), calls=%async_computation | async-start | bytes 1228800 | tf_op jit(solution)/shard_map/psum | solution.py:390
  74.5 7.2 %copy-start.6 = (bf16[2,197,384]{2,0,1:T(2,128)(2,1)S(1)}, bf16[2,197,384]{2,0,1:T(2,128)(2,1)}, u32[]{:S(2)}) copy-start(bf16[2,197,384]{2,0,1:T(2,128)(2,1)} %param.12) | copy-start | bytes 907780
  81.3 3.8 copy-start.33
  81.7 3.4 copy-start.44
  87.4 3.6 copy-start.29
  88.6 13.8 %copy-start.32 = (s32[1,2,197,2]{2,3,1,0:T(2,128)S(1)}, s32[1,2,197,2]{2,3,1,0:T(2,128)}, u32[]{:S(2)}) copy-start(s32[1,2,197,2]{2,3,1,0:T(2,128)} %param.13) | copy-start | bytes 9460
  89.4 13.0 %copy-start.22 = (bf16[64,192,6]{0,2,1:T(8,128)(2,1)}, bf16[64,192,6]{0,2,1:T(8,128)(2,1)S(1)}, u32[]{:S(2)}) copy-start(bf16[64,192,6]{0,2,1:T(8,128)(2,1)S(1)} %reshape.488) | copy-start | bytes 442372
  91.1 205.9 %all-reduce.12.cloned.1.call-start = ((), (), s32[]{:S(2)}) async-start(), calls=%async_computation.1 | async-start | bytes 1228800 | tf_op jit(solution)/shard_map/psum | solution.py:460
  123.9 7.4 %copy-start.53 = (s32[788]{0:T(1024)}, s32[788]{0:T(1024)S(1)}, u32[]{:S(2)}) copy-start(s32[788]{0:T(1024)S(1)} %fusion.89) | copy-start | bytes 9460
  131.6 36.8 %copy-start.36 = (f32[384]{0:T(512)}, f32[384]{0:T(512)S(1)}, u32[]{:S(2)}) copy-start(f32[384]{0:T(512)S(1)} %mul.252) | copy-start | bytes 4612
  144.4 9.5 %copy-start.28 = (bf16[2,197,384]{2,0,1:T(2,128)(2,1)S(1)}, bf16[2,197,384]{2,0,1:T(2,128)(2,1)}, u32[]{:S(2)}) copy-start(bf16[2,197,384]{2,0,1:T(2,128)(2,1)} %param.21) | copy-start | bytes 907780
  157.6 41.4 %copy-start.35 = (s32[1024]{0:T(1024)}, s32[1024]{0:T(1024)S(1)}, u32[]{:S(2)}) copy-start(s32[1024]{0:T(1024)S(1)} %get-tuple-element.102) | copy-start | bytes 12292
  174.0 3.2 copy-start.50
  187.2 4.7 %copy-start.24 = (bf16[2,4,104,768]{3,2,0,1:T(8,128)(2,1)}, bf16[2,4,104,768]{3,2,0,1:T(8,128)(2,1)S(1)}, u32[]{:S(2)}) copy-start(bf16[2,4,104,768]{3,2,0,1:T(8,128)(2,1)S(1)} %get-tuple-element.95) | copy-start | bytes 3833860
  199.0 3.4 copy-start.47
  202.5 15.9 %copy-start.40 = (f32[394,4]{0,1:T(4,128)S(1)}, f32[394,4]{0,1:T(4,128)}, u32[]{:S(2)}) copy-start(f32[394,4]{0,1:T(4,128)} %fusion.84) | copy-start | bytes 18916
  202.5 15.9 %copy-start.46 = (s32[394,2]{0,1:T(2,128)S(1)}, s32[394,2]{0,1:T(2,128)}, u32[]{:S(2)}) copy-start(s32[394,2]{0,1:T(2,128)} %eq.30) | copy-start | bytes 9460
  202.5 22.8 %copy-start.51 = (pred[2,4,104]{2,1,0:T(4,128)(4,1)S(1)}, pred[2,4,104]{2,1,0:T(4,128)(4,1)}, u32[]{:S(2)}) copy-start(pred[2,4,104]{2,1,0:T(4,128)(4,1)} %broadcast_in_dim.49) | copy-start | bytes 2500
  219.2 10.4 %copy-start.12 = (f32[394,2]{1,0:T(8,128)}, f32[394,2]{1,0:T(8,128)S(1)}, u32[]{:S(2)}) copy-start(f32[394,2]{1,0:T(8,128)S(1)} %copy.307) | copy-start | bytes 9460
  225.2 4.3 copy-start.4
  225.2 4.3 copy-start.55
  229.5 5.4 %copy-start.8 = (bf16[64,4,6,768]{3,2,1,0:T(8,128)(2,1)S(1)}, bf16[64,4,6,768]{3,2,1,0:T(8,128)(2,1)}, u32[]{:S(2)}) copy-start(bf16[64,4,6,768]{3,2,1,0:T(8,128)(2,1)} %reshape.490) | copy-start | bytes 7077892
  234.9 2.7 copy-start.54
  250.0 5.7 %copy-start.43 = (f32[394]{0:T(512)S(1)}, f32[394]{0:T(512)}, u32[]{:S(2)}) copy-start(f32[394]{0:T(512)} %multiply_reduce_fusion.8) | copy-start | bytes 4732
  251.8 4.1 copy-start.5
  255.4 98.4 %all-reduce.14.cloned.1.call-start = ((), (), s32[]{:S(2)}) async-start(), calls=%async_computation.2 | async-start | bytes 1228800 | tf_op jit(solution)/shard_map/psum | solution.py:419
  277.8 6.0 %copy-start.25 = (bf16[2,4,104,64,6]{2,1,0,4,3:T(4,128)(2,1)S(1)}, bf16[2,4,104,64,6]{2,1,0,4,3:T(4,128)(2,1)}, u32[]{:S(2)}) copy-start(bf16[2,4,104,64,6]{2,1,0,4,3:T(4,128)(2,1)} %gather.26) | copy-start | bytes 1916932
  277.8 6.0 %copy-start.52 = (pred[2,4,104]{2,1,0:T(4,128)(4,1)S(1)}, pred[2,4,104]{2,1,0:T(4,128)(4,1)}, u32[]{:S(2)}) copy-start(pred[2,4,104]{2,1,0:T(4,128)(4,1)} %broadcast_in_dim.49) | copy-start | bytes 2500
  289.1 5.7 %copy-start.7 = (f32[394,2,384]{2,1,0:T(2,128)S(1)}, f32[394,2,384]{2,1,0:T(2,128)}, u32[]{:S(2)}) copy-start(f32[394,2,384]{2,1,0:T(2,128)} %reshape.495) | copy-start | bytes 3631108
  289.1 5.7 %copy-start.13 = (f32[394,2]{1,0:T(8,128)S(1)}, f32[394,2]{1,0:T(8,128)}, u32[]{:S(2)}) copy-start(f32[394,2]{1,0:T(8,128)} %copy-done.12) | copy-start | bytes 9460
  289.1 7.9 %copy-start.37 = (f32[384]{0:T(512)S(1)}, f32[384]{0:T(512)}, u32[]{:S(2)}) copy-start(f32[384]{0:T(512)} %copy-done.36) | copy-start | bytes 4612
  289.1 7.9 %copy-start.39 = (f32[394]{0:T(512)S(1)}, f32[394]{0:T(512)}, u32[]{:S(2)}) copy-start(f32[394]{0:T(512)} %copy-done.38) | copy-start | bytes 4732
  299.2 3.4 copy-start.23
  299.2 4.9 %copy-start.1 = (f32[2,3,197,197]{2,3,1,0:T(8,128)S(1)}, f32[2,3,197,197]{2,3,1,0:T(8,128)}, u32[]{:S(2)}) copy-start(f32[2,3,197,197]{2,3,1,0:T(8,128)} %copy-done) | copy-start | bytes 2794252
  299.2 5.0 %copy-start.30 = (f32[2,3,197]{2,1,0:T(4,128)S(1)}, f32[2,3,197]{2,1,0:T(4,128)}, u32[]{:S(2)}) copy-start(f32[2,3,197]{2,1,0:T(4,128)} %copy-done.29) | copy-start | bytes 14188
  300.4 4.1 copy-start.15
  306.1 2.4 copy-start.31
  307.2 3.3 copy-start.34
  307.2 3.3 copy-start.41
  307.3 3.3 copy-start.42
  307.3 3.3 copy-start.45
  313.7 4.0 copy-start.3
  427.1 12.8 %copy-start.10 = (f32[336,128]{1,0:T(8,128)}, f32[336,128]{1,0:T(8,128)S(1)}, u32[]{:S(2)}) copy-start(f32[336,128]{1,0:T(8,128)S(1)} %add.237) | copy-start | bytes 516100
  432.2 7.7 %slice-start = ((f32[1792,6,4]{2,1,0:T(8,128)}), f32[1,6,4]{2,1,0:T(8,128)S(1)}, s32[]{:S(2)}) async-start(f32[1792,6,4]{2,1,0:T(8,128)} %add.238), calls=%async_computation.3 | async-start | bytes 8192 | tf_op jit(solution)/shard_map/slice | solution.py:354
  439.8 9.4 %copy-start.9 = (bf16[394,384]{1,0:T(8,128)(2,1)S(1)}, bf16[394,384]{1,0:T(8,128)(2,1)}, u32[]{:S(2)}) copy-start(bf16[394,384]{1,0:T(8,128)(2,1)} %get-tuple-element.69) | copy-start | bytes 907780
  439.8 9.4 %copy-start.11 = (f32[394,384]{1,0:T(8,128)S(1)}, f32[394,384]{1,0:T(8,128)}, u32[]{:S(2)}) copy-start(f32[394,384]{1,0:T(8,128)} %get-tuple-element.71) | copy-start | bytes 1815556
  439.9 8.7 %slice-start.1 = ((f32[336,128]{1,0:T(8,128)}), f32[27,128]{1,0:T(8,128)S(1)}, s32[]{:S(2)}) async-start(f32[336,128]{1,0:T(8,128)} %copy-done.10), calls=%async_computation.4 | async-start | bytes 32768 | tf_op jit(solution)/shard_map/slice | solution.py:354
  447.1 3.7 copy-start.27
  (13 other events, 20.8 us)
Sparse Core Ops, SparseCore 0:
  91.2 41.3 all-reduce.9
  255.5 39.8 all-reduce.11
  313.8 40.0 all-reduce.13
where the time goes:
time: 464 us; the launch traced here: 459 us
  local copies, waits for them, and re-layouts  204 us (44%)
  Pallas kernels  117 us (25%)
  matrix products  39.9 us (9%)
  waiting for transfers between devices  32.8 us (7%)
  other arithmetic  25.1 us (5%)
  between operations  15.5 us (3%)
  blocking collectives  12.7 us (3%)
  starting transfers between devices  11.5 us (2%)
    pallas_call x1, Pallas kernels, relay_gather(): pl.pallas_call(functools.partial(relay_gather_kernel, chips, direct), out...  58.9 us
    pallas_call x1, Pallas kernels, relay_reduce(): pl.pallas_call(functools.partial(relay_reduce_kernel, chips, direct), out...  58.5 us
    unnamed x139, local copies, waits for them, and re-layouts  34.7 us
    psum x1, waiting for transfers between devices, layer_forward(): lax.psum(partial_moe.astype(jnp.bfloat16), 'mp').astype(jnp.float32)  32.7 us
    reshape x3, local copies, waits for them, and re-layouts, gather_weights(): pieces.append(full[:, start:start + a.size].reshape((n,) + a.shape[1:]))  15.7 us
    reshape x2, local copies, waits for them, and re-layouts, scatter_grads(): go.reshape(n, -1)  15.5 us
    gather x3, local copies, waits for them, and re-layouts, slot_positions(): return jnp.take_along_axis(before, chosen_ids, axis=-1)  12.9 us
    add x2, local copies, waits for them, and re-layouts, relay_reduce(): jnp.sum(same.astype(jnp.float32), axis=0)  12.7 us
  transfers between devices with their start and end apart: 3, of which 1 were waited for; matrix products, arithmetic and copies ran while one was open for 25% of the time, Pallas kernels for 0%

commit v1 on v0

--- a/solution.py
+++ b/solution.py
@@ -510,7 +510,8 @@
     partial_first = jnp.einsum(
         "rcf,dcf->rd", grad_projected, w_qkv, preferred_element_type=jnp.float32
     )
-    grad_first = lax.psum(partial_first.astype(jnp.bfloat16), "mp").astype(jnp.float32)
+    both = exchange(partial_first.astype(jnp.bfloat16), 2, True, "pair", 2).astype(jnp.float32)
+    grad_first = (both[0] + both[1]).astype(jnp.bfloat16).astype(jnp.float32)
     grad_input_norm, grad_gain_one, grad_shift_one = norm_backward(
         grad_first, normed_one, inverse_one, gain_rows[0]
     )

time: 464 us -> 469 us (1.011)
  Pallas kernels: 117 us -> 129 us
    pallas_call x0 -> x1, Pallas kernels: none -> 10.5 us  [exchange(): pl.pallas_call(functools.partial(exchange_kernel, m, pieces, gather, kind...]
    unnamed x139 -> x145, local copies, waits for them, and re-layouts: 34.7 us -> 34.2 us
  transfers between devices with their start and end apart: 3 -> 3, of which waited for: 1 -> 1; matrix products, arithmetic and copies ran while one was open for 25% -> 23% of each run, Pallas kernels for 0% -> 0%
where the time goes in v1:
time: 469 us; the launch traced here: 464 us
  local copies, waits for them, and re-layouts  202 us (43%)
  Pallas kernels  129 us (28%)
  matrix products  37.6 us (8%)
  waiting for transfers between devices  31.3 us (7%)
  other arithmetic  24.5 us (5%)
  between operations  15.6 us (3%)
  blocking collectives  12.6 us (3%)
  starting transfers between devices  11.5 us (2%)
    pallas_call x1, Pallas kernels, relay_reduce(): pl.pallas_call(functools.partial(relay_reduce_kernel, chips, direct), out...  59.1 us
    pallas_call x1, Pallas kernels, relay_gather(): pl.pallas_call(functools.partial(relay_gather_kernel, chips, direct), out...  58.9 us
    unnamed x145, local copies, waits for them, and re-layouts  34.2 us
    psum x1, waiting for transfers between devices, layer_forward(): lax.psum(partial_moe.astype(jnp.bfloat16), 'mp').astype(jnp.float32)  31.2 us
    reshape x3, local copies, waits for them, and re-layouts, gather_weights(): pieces.append(full[:, start:start + a.size].reshape((n,) + a.shape[1:]))  15.7 us
    reshape x2, local copies, waits for them, and re-layouts, scatter_grads(): go.reshape(n, -1)  15.5 us
    gather x3, local copies, waits for them, and re-layouts, slot_positions(): return jnp.take_along_axis(before, chosen_ids, axis=-1)  12.9 us
    add x2, local copies, waits for them, and re-layouts, relay_reduce(): jnp.sum(same.astype(jnp.float32), axis=0)  12.7 us
  transfers between devices with their start and end apart: 3, of which 1 were waited for; matrix products, arithmetic and copies ran while one was open for 23% of the time, Pallas kernels for 0%

profile of v1, /device:TPU:1, one launch (start us, length us, event | category | flops | bytes accessed | tf_op | source)
XLA Modules:
  0.0 463.9 jit_solution(11203948765734203738)
XLA Ops:
  15.5 58.9 %shard_map.169 = bf16[64,336,128]{2,1,0:T(8,128)(2,1)} custom-call(bf16[336,128]{1,0:T(8,128)(2,1)} %pad_bitcast_fusion.1.x_ref), custom_call_target="tpu_custom_call" | custom-call | bytes 11010048 | tf_op jit(solution)/shard_map/pallas_call | solution.py:202
  74.5 4.0 copy.476
  78.7 2.3 copy-done.2
  91.4 11.3 %all-reduce.13.cloned.1.call-start = ((), (), s32[]{:S(2)}) async-start(), calls=%async_computation.2 | async-start | bytes 1228800 | tf_op jit(solution)/shard_map/psum | solution.py:460
  102.9 5.0 %fusion.100 = (bf16[64,18432]{1,0:T(8,128)(2,1)}, bf16[64,18432]{1,0:T(8,128)(2,1)}) fusion(bf16[64,43008]{1,0:T(8,128)(2,1)} %bitcast.233), kind=kLoop, calls=%fused_computation.194 | loop fusion | bytes 9437184 | tf_op jit(solution)/shard_map/slice | solution.py:322
  107.9 2.4 reduce-window.6
  111.7 12.6 %gather_fusion.2 = s32[788]{0:T(1024)S(1)} fusion(s32[2,197,4]{1,2,0:T(4,128)S(1)} %slice_subtract_fusion, s32[788]{0:T(1024)S(1)} %reshape.555), kind=kCustom, calls=%fused_computation.4 | custom fusion | bytes 15760 | tf_op jit(solution)/shard_map/jit(take_along_axis)/gather | solution.py:44
  124.4 5.3 %scatter_custom_fusion = s32[832]{0:T(1024)S(1)} fusion(s32[788]{0:T(1024)S(1)} %fusion.90, s32[788]{0:T(1024)S(1)} %reshape.565, s32[]{:T(128)} %constant.38.clone.1), kind=kCustom, calls=%fused_computation.182 | custom fusion | bytes 3332 | tf_op jit(solution)/shard_map/scatter | solution.py:405
  135.2 3.4 gather_fusion.1
  140.4 2.9 gather.29
  143.7 1.9 mul.280
  146.2 6.1 %reshape.493 = bf16[64,4,6,768]{3,2,1,0:T(8,128)(2,1)} reshape(bf16[64,18432]{1,0:T(8,128)(2,1)} %get-tuple-element.78) | data formatting | bytes 4718592 | tf_op jit(solution)/shard_map/reshape | solution.py:322
  152.3 5.7 %copy.312 = bf16[64,18432]{0,1:T(8,128)(2,1)} copy(bf16[64,18432]{1,0:T(8,128)(2,1)} %get-tuple-element.79) | data formatting | bytes 4718592 | tf_op jit(solution)/shard_map/slice | solution.py:322
  158.0 9.4 %reshape.492 = bf16[64,4,768,6]{0,3,2,1:T(8,128)(2,1)} reshape(bf16[64,18432]{0,1:T(8,128)(2,1)} %copy.312) | data formatting | bytes 4718592 | tf_op jit(solution)/shard_map/reshape | solution.py:322
  170.7 3.9 gather_fusion
  177.8 10.0 %fusion.6 = (bf16[2,4,104,768]{3,2,0,1:T(8,128)(2,1)S(1)}, f32[4,768,2,104,1]{1,3,4,2,0:T(8,128)}) fusion(bf16[64,4,6,768,1]{3,2,1,0,4:T(8,128)(2,1)} %bitcast.240, bf16[2,4,104,64,6]{2,1,0,4,3:T(4,128)(2,1)} %gather.26, pred[2,4,104]{2,1,0:T(4,128)(4,1)S(1)} %copy-done.52), kind=kOutput, calls=%fused_computation.20 | convolution fusion | flops 532586496 | bytes 6832960 | tf_op jit(solution)/shard_map/becjk,jekf->becf/dot_general | solution.py:413
  187.8 4.7 %fusion.37 = f32[2,4,104,64,6]{2,3,0,4,1:T(8,128)S(1)} fusion(bf16[64,4,768,6,1]{0,3,2,1,4:T(8,128)(2,1)} %bitcast.236, bf16[2,4,104,768]{3,2,0,1:T(8,128)(2,1)S(1)} %get-tuple-element.96), kind=kOutput, calls=%fused_computation.59 | convolution fusion | flops 490733568 | bytes 4915200 | tf_op jit(solution)/shard_map/becf,jefk->becjk/dot_general | solution.py:415
  192.5 2.2 copy.319
  194.6 3.2 reshape.497
  199.6 3.4 gather_fusion.3
  203.0 2.9 multiply_reduce_fusion.1
  206.1 12.6 %psum.31 = f32[394,2]{1,0:T(8,128)S(1)} all-reduce(f32[394,2]{1,0:T(8,128)S(1)} %reduce_sum.229), channel_id=1, replica_groups=mesh['dp'=64,'mp'=2] {'mp'}, use_global_device_ids=true, to_apply=%region_20.22 | all-reduce | flops 788 | bytes 6304 | tf_op jit(solution)/shard_map/psum | solution.py:460
  219.9 5.8 %scatter_custom_fusion.1 = f32[832]{0:T(1024)S(1)} fusion(s32[788]{0:T(1024)} %copy-done.55, f32[788]{0:T(1024)S(1)} %reshape.573, f32[]{:T(128)} %constant.56.clone.1), kind=kCustom, calls=%fused_computation.180 | custom fusion | bytes 3840 | tf_op jit(solution)/shard_map/scatter | solution.py:408
  225.8 4.3 fusion.47
  230.1 5.4 %fusion.43 = bf16[2,4,104,768,1]{3,2,0,4,1:T(8,128)(2,1)S(1)} fusion(f32[4,768,2,104,1]{1,3,4,2,0:T(8,128)S(1)} %copy-done.58, bf16[64,4,768,6,1]{0,3,2,1,4:T(8,128)(2,1)} %bitcast.237, f32[2,4,104,64,6]{2,1,0,4,3:T(4,128)S(1)} %copy-done.4, f32[2,4,104]{2,1,0:T(4,128)S(1)} %mul.267, pred[2,4,104]{2,1,0:T(4,128)(4,1)S(1)} %copy-done.53), kind=kOutput, calls=%fused_computation.61 | convolution fusion | flops 498081792 | bytes 7475264 | tf_op jit(solution)/shard_map/becjk,jefk->becf/dot_general | solution.py:447
  235.5 2.7 fusion.40
  238.2 2.2 copy.328
  240.4 3.3 reshape.503
  245.4 3.7 gather_fusion.4
  252.3 3.6 reduce_sum.227
  257.3 3.4 copy.477
  261.6 3.0 copy.347
  264.5 5.6 %reshape.510 = bf16[64,18432]{1,0:T(8,128)(2,1)} reshape(bf16[64,4,6,768]{3,2,1,0:T(8,128)(2,1)} %copy.347) | data formatting | bytes 4718592 | tf_op jit(solution)/shard_map/reshape | solution.py:337
  271.9 6.9 %copy.349 = bf16[64,4,768,6]{0,3,2,1:T(8,128)(2,1)} copy(bf16[64,4,768,6]{2,0,3,1:T(8,128)(2,1)} %bitcast.235) | data formatting | bytes 4718592 | tf_op jit(solution)/shard_map/becf,becjk->jefk/transpose | solution.py:444
  278.8 9.5 %reshape.511 = bf16[64,18432]{0,1:T(8,128)(2,1)} reshape(bf16[64,4,768,6]{0,3,2,1:T(8,128)(2,1)} %copy.349) | data formatting | bytes 4718592 | tf_op jit(solution)/shard_map/reshape | solution.py:338
  288.3 6.0 %copy.358 = bf16[64,18432]{1,0:T(8,128)(2,1)} copy(bf16[64,18432]{0,1:T(8,128)(2,1)} %reshape.511) | data formatting | bytes 4718592 | tf_op jit(solution)/shard_map/reshape | solution.py:338
  294.3 2.2 multiply_reduce_fusion.2
  296.6 2.2 multiply_reduce_fusion.3
  298.9 31.2 %all-reduce.11.cloned.1.call-done = bf16[394,384]{1,0:T(8,128)(2,1)} async-done(((bf16[394,384]{1,0:T(8,128)(2,1)}), bf16[394,384]{1,0:T(8,128)(2,1)}) %all-reduce.11.cloned.1.call-update) | async-done | bytes 302608 | tf_op jit(solution)/shard_map/psum | solution.py:419
  330.1 2.5 fusion.98
  342.6 10.5 %shard_map.170 = bf16[2,394,384]{2,1,0:T(8,128)(2,1)} custom-call(bf16[394,384]{1,0:T(8,128)(2,1)} %fusion.49.x_ref), custom_call_target="tpu_custom_call" | custom-call | bytes 1210368 | tf_op jit(solution)/shard_map/pallas_call | solution.py:122
  357.8 3.2 constant_dynamic-update-slice_fusion.4
  367.0 2.9 pad_bitcast_fusion
  369.9 3.3 copy.398
  373.2 59.1 %shard_map.171 = (bf16[32,336,128]{2,1,0:T(8,128)(2,1)}, bf16[8,336,128]{2,1,0:T(8,128)(2,1)}) custom-call(bf16[64,336,128]{2,1,0:T(8,128)(2,1)} %bitcast.228), custom_call_target="tpu_custom_call" | custom-call | bytes 16515072 | tf_op jit(solution)/shard_map/pallas_call | solution.py:286
  432.3 2.2 convert_reduce_fusion
  434.7 7.7 %add.242 = f32[3584,2,6]{2,1,0:T(2,128)} reshape(f32[336,128]{1,0:T(8,128)S(1)} %add.240) | data formatting | bytes 344064 | tf_op jit(solution)/shard_map/add | solution.py:300
  442.4 5.0 %add.241 = f32[1792,6,4]{2,1,0:T(8,128)} reshape(f32[336,128]{1,0:T(8,128)S(1)} %add.240) | data formatting | bytes 344064 | tf_op jit(solution)/shard_map/add | solution.py:300
  (329 shorter events, 76.6 us)
Async XLA Ops:
  7.2 160.3 %all-reduce.9.cloned.1.call-start = ((), (), s32[]{:S(2)}) async-start(), calls=%async_computation | async-start | bytes 1228800 | tf_op jit(solution)/shard_map/psum | solution.py:390
  74.5 6.5 %copy-start.6 = (bf16[2,197,384]{2,0,1:T(2,128)(2,1)S(1)}, bf16[2,197,384]{2,0,1:T(2,128)(2,1)}, u32[]{:S(2)}) copy-start(bf16[2,197,384]{2,0,1:T(2,128)(2,1)} %param.12) | copy-start | bytes 907780
  78.5 2.4 copy-start.2
  82.5 2.9 copy-start.46
  82.8 2.7 copy-start.35
  88.0 2.2 copy-start.15
  88.0 2.2 copy-start.17
  88.5 14.2 %copy-start.34 = (s32[1,2,197,2]{2,3,1,0:T(2,128)S(1)}, s32[1,2,197,2]{2,3,1,0:T(2,128)}, u32[]{:S(2)}) copy-start(s32[1,2,197,2]{2,3,1,0:T(2,128)} %param.13) | copy-start | bytes 9460
  88.7 19.2 %copy-start.30 = (f32[2,3,197]{2,1,0:T(4,128)}, f32[2,3,197]{2,1,0:T(4,128)S(1)}, u32[]{:S(2)}) copy-start(f32[2,3,197]{2,1,0:T(4,128)S(1)} %log_add_fusion) | copy-start | bytes 14188
  91.4 205.2 %all-reduce.13.cloned.1.call-start = ((), (), s32[]{:S(2)}) async-start(), calls=%async_computation.2 | async-start | bytes 1228800 | tf_op jit(solution)/shard_map/psum | solution.py:460
  111.7 22.7 %copy-start.29 = (bf16[2,197,384]{2,0,1:T(2,128)(2,1)S(1)}, bf16[2,197,384]{2,0,1:T(2,128)(2,1)}, u32[]{:S(2)}) copy-start(bf16[2,197,384]{2,0,1:T(2,128)(2,1)} %param.21) | copy-start | bytes 907780
  124.3 5.3 %copy-start.55 = (s32[788]{0:T(1024)}, s32[788]{0:T(1024)S(1)}, u32[]{:S(2)}) copy-start(s32[788]{0:T(1024)S(1)} %fusion.90) | copy-start | bytes 9460
  135.2 64.4 %copy-start.37 = (s32[1024]{0:T(1024)}, s32[1024]{0:T(1024)S(1)}, u32[]{:S(2)}) copy-start(s32[1024]{0:T(1024)S(1)} %get-tuple-element.103) | copy-start | bytes 12292
  146.0 22.9 %copy-start.38 = (f32[384]{0:T(512)}, f32[384]{0:T(512)S(1)}, u32[]{:S(2)}) copy-start(f32[384]{0:T(512)S(1)} %mul.252) | copy-start | bytes 4612
  174.6 3.2 copy-start.52
  187.8 4.7 %copy-start.25 = (bf16[2,4,104,768]{3,2,0,1:T(8,128)(2,1)}, bf16[2,4,104,768]{3,2,0,1:T(8,128)(2,1)S(1)}, u32[]{:S(2)}) copy-start(bf16[2,4,104,768]{3,2,0,1:T(8,128)(2,1)S(1)} %get-tuple-element.96) | copy-start | bytes 3833860
  199.6 3.4 copy-start.49
  203.0 15.9 %copy-start.42 = (f32[394,4]{0,1:T(4,128)S(1)}, f32[394,4]{0,1:T(4,128)}, u32[]{:S(2)}) copy-start(f32[394,4]{0,1:T(4,128)} %fusion.85) | copy-start | bytes 18916
  203.0 15.9 %copy-start.48 = (s32[394,2]{0,1:T(2,128)S(1)}, s32[394,2]{0,1:T(2,128)}, u32[]{:S(2)}) copy-start(s32[394,2]{0,1:T(2,128)} %eq.30) | copy-start | bytes 9460
  203.0 22.7 %copy-start.53 = (pred[2,4,104]{2,1,0:T(4,128)(4,1)S(1)}, pred[2,4,104]{2,1,0:T(4,128)(4,1)}, u32[]{:S(2)}) copy-start(pred[2,4,104]{2,1,0:T(4,128)(4,1)} %broadcast_in_dim.49) | copy-start | bytes 2500
  219.7 10.4 %copy-start.13 = (f32[394,2]{1,0:T(8,128)}, f32[394,2]{1,0:T(8,128)S(1)}, u32[]{:S(2)}) copy-start(f32[394,2]{1,0:T(8,128)S(1)} %copy.307) | copy-start | bytes 9460
  225.8 4.3 copy-start.4
  225.8 4.3 copy-start.58
  230.1 5.4 %copy-start.8 = (bf16[64,4,6,768]{3,2,1,0:T(8,128)(2,1)S(1)}, bf16[64,4,6,768]{3,2,1,0:T(8,128)(2,1)}, u32[]{:S(2)}) copy-start(bf16[64,4,6,768]{3,2,1,0:T(8,128)(2,1)} %reshape.493) | copy-start | bytes 7077892
  235.5 2.7 copy-start.56
  250.6 5.6 %copy-start.45 = (f32[394]{0:T(512)S(1)}, f32[394]{0:T(512)}, u32[]{:S(2)}) copy-start(f32[394]{0:T(512)} %multiply_reduce_fusion.8) | copy-start | bytes 4732
  256.0 4.8 %copy-start.26 = (bf16[2,4,104,64,6]{2,1,0,4,3:T(4,128)(2,1)S(1)}, bf16[2,4,104,64,6]{2,1,0,4,3:T(4,128)(2,1)}, u32[]{:S(2)}) copy-start(bf16[2,4,104,64,6]{2,1,0,4,3:T(4,128)(2,1)} %gather.26) | copy-start | bytes 1916932
  256.0 4.7 %copy-start.54 = (pred[2,4,104]{2,1,0:T(4,128)(4,1)S(1)}, pred[2,4,104]{2,1,0:T(4,128)(4,1)}, u32[]{:S(2)}) copy-start(pred[2,4,104]{2,1,0:T(4,128)(4,1)} %broadcast_in_dim.49) | copy-start | bytes 2500
  256.0 74.1 %all-reduce.11.cloned.1.call-start = ((), (), s32[]{:S(2)}) async-start(), calls=%async_computation.1 | async-start | bytes 614400 | tf_op jit(solution)/shard_map/psum | solution.py:419
  257.3 3.4 copy-start.57
  264.5 5.6 %copy-start.5 = (f32[788,384]{1,0:T(8,128)S(1)}, f32[788,384]{1,0:T(8,128)}, u32[]{:S(2)}) copy-start(f32[788,384]{1,0:T(8,128)} %get-tuple-element.73) | copy-start | bytes 3631108
  288.3 6.0 %copy-start.7 = (f32[394,2,384]{2,1,0:T(2,128)S(1)}, f32[394,2,384]{2,1,0:T(2,128)}, u32[]{:S(2)}) copy-start(f32[394,2,384]{2,1,0:T(2,128)} %reshape.498) | copy-start | bytes 3631108
  288.3 6.0 %copy-start.14 = (f32[394,2]{1,0:T(8,128)S(1)}, f32[394,2]{1,0:T(8,128)}, u32[]{:S(2)}) copy-start(f32[394,2]{1,0:T(8,128)} %copy-done.13) | copy-start | bytes 9460
  288.3 8.3 %copy-start.39 = (f32[384]{0:T(512)S(1)}, f32[384]{0:T(512)}, u32[]{:S(2)}) copy-start(f32[384]{0:T(512)} %copy-done.38) | copy-start | bytes 4612
  288.3 8.3 %copy-start.41 = (f32[394]{0:T(512)S(1)}, f32[394]{0:T(512)}, u32[]{:S(2)}) copy-start(f32[394]{0:T(512)} %copy-done.40) | copy-start | bytes 4732
  330.1 4.0 copy-start.24
  332.6 2.4 copy-start.1
  332.6 2.4 copy-start.31
  332.6 2.7 copy-start.16
  339.6 2.2 copy-start.36
  339.7 2.2 copy-start.43
  339.7 2.2 copy-start.44
  339.7 2.2 copy-start.47
  357.0 4.0 copy-start.3
  432.3 2.3 copy-start.27
  434.7 12.7 %copy-start.9 = (f32[336,128]{1,0:T(8,128)}, f32[336,128]{1,0:T(8,128)S(1)}, u32[]{:S(2)}) copy-start(f32[336,128]{1,0:T(8,128)S(1)} %add.240) | copy-start | bytes 516100
  442.4 5.0 %copy-start.11 = (f32[394,384]{1,0:T(8,128)S(1)}, f32[394,384]{1,0:T(8,128)}, u32[]{:S(2)}) copy-start(f32[394,384]{1,0:T(8,128)} %get-tuple-element.84) | copy-start | bytes 1815556
  449.0 7.3 %slice-start = ((f32[1792,6,4]{2,1,0:T(8,128)}), f32[1,6,4]{2,1,0:T(8,128)S(1)}, s32[]{:S(2)}) async-start(f32[1792,6,4]{2,1,0:T(8,128)} %add.241), calls=%async_computation.3 | async-start | bytes 8192 | tf_op jit(solution)/shard_map/slice | solution.py:354
  (16 other events, 20.1 us)
Sparse Core Ops, SparseCore 0:
  91.5 41.3 all-reduce.8
  256.1 39.8 all-reduce.12
  298.4 31.6 all-reduce.10
